TPU v7x, 256 devices: a whole 4x4x8 slice. The times are simulated.
256 devices in a mesh: batch: 16 (over z, core), proto: 16 (over x, y).
Axes of the slice: x: 4, y: 4, z: 8, core: 2. Of those that a mesh axis runs over, the one named last changes fastest.
Arguments:
- slow_embed: bfloat16 [16384, 256], P('batch'), may hold values from -1 to 1
- fast_embed: bfloat16 [16384, 256], P('batch'), may hold values from -1 to 1
- prototypes: float32 [32768, 256], P('proto'), may hold values from -1 to 1
Outputs:
- proto_grad: float32 [32768, 256], P('proto')
- slow_grad: float32 [16384, 256], P('batch')
- fast_grad: float32 [16384, 256], P('batch')
All inputs are finite; a program needn't handle non-finite values.
Results may differ from a plain program's by a relative error of at most 0.0005.
The roundings to bfloat16 on the way count: a program that leaves them out, or rounds other values in their place, can miss the bound.
Values sent between devices are 32-bit elements; how exact they have to be, the bound alone decides.
A program may use at most 128 MiB of HBM per device.

v0:
```python
import jax
import jax.numpy as jnp
from jax import lax
from jax.sharding import PartitionSpec as P

ITERS = 3
CODE_EPS = 0.05
TEMPER = 0.1
NORM_EPS = 1e-06


def normalize(raw_rows):
    lengths = jnp.sqrt(jnp.sum(raw_rows * raw_rows, axis=-1, keepdims=True) + 1e-12)
    return (raw_rows / lengths, lengths)


def project_back(grad_unit, unit_vec, lengths):
    along = jnp.sum(unit_vec * grad_unit, axis=-1, keepdims=True)
    return (grad_unit - unit_vec * along) / lengths


def row_total(row_terms):
    return lax.psum(row_terms, "proto")


def normalizers(proto_square, embed_square, proto_entries, embed_entries):
    totals = lax.psum((proto_square, embed_square), ("batch", "proto"))
    proto_factor = lax.rsqrt(totals[0] / proto_entries + NORM_EPS)
    embed_factor = lax.rsqrt(totals[1] / embed_entries + NORM_EPS)
    return (proto_factor, embed_factor)


def body(slow_embed, fast_embed, prototypes):
    clip_dev = slow_embed.shape[0]
    proto_dev = prototypes.shape[0]
    feat_width = prototypes.shape[1]
    batch_count = lax.axis_size("batch")
    proto_count = lax.axis_size("proto")
    clips_all = clip_dev * batch_count
    protos_all = proto_dev * proto_count
    proto_entries = float(protos_all * feat_width)
    embed_entries = float(2 * clips_all * feat_width)
    raw_views = jnp.stack([slow_embed, fast_embed]).astype(jnp.float32)
    unit_vec, lengths = normalize(raw_views)
    unit_b = unit_vec.astype(jnp.bfloat16)
    proto_unit, proto_len = normalize(prototypes)
    proto_b = proto_unit.astype(jnp.bfloat16)
    scores = jnp.einsum("vbd,kd->vbk", unit_b, proto_b, preferred_element_type=jnp.float32)
    code_table = jnp.exp(scores / CODE_EPS)
    soft_exp = jnp.exp(scores / TEMPER)
    denom_terms = jnp.sum(soft_exp, axis=2)
    denominator = lax.psum(denom_terms, "proto")
    clip_scale = jnp.ones((2, clip_dev), jnp.float32)
    for iteration in range(ITERS):
        col_total = lax.psum(jnp.sum(code_table * clip_scale[:, :, None], axis=1), "batch")
        proto_scale = 1.0 / (protos_all * col_total)
        row_terms = jnp.sum(code_table * proto_scale[:, None, :], axis=2)
        if iteration == 0:
            clip_total = row_total(row_terms)
        else:
            clip_total = row_total(row_terms)
        clip_scale = 1.0 / (clips_all * clip_total)
    codes = code_table * proto_scale[:, None, :] / clip_total[:, :, None]
    probs = soft_exp / denominator[:, :, None]
    score_grad = (jnp.stack([probs[0] - codes[1], probs[1] - codes[0]]) / TEMPER).astype(
        jnp.bfloat16
    )
    proto_terms = jnp.einsum("vbk,vbd->kd", score_grad, unit_b, preferred_element_type=jnp.float32)
    grad_proto_unit = lax.psum(proto_terms, "batch")
    embed_terms = jnp.einsum("vbk,kd->vbd", score_grad, proto_b, preferred_element_type=jnp.float32)
    grad_unit = lax.psum(embed_terms, "proto")
    grad_proto = project_back(grad_proto_unit, proto_unit, proto_len)
    grad_embed = project_back(grad_unit, unit_vec, lengths)
    proto_factor, embed_factor = normalizers(
        jnp.sum(grad_proto * grad_proto) / batch_count,
        jnp.sum(grad_embed * grad_embed) / proto_count,
        proto_entries,
        embed_entries,
    )
    proto_grad = grad_proto * proto_factor
    slow_grad = grad_embed[0] * embed_factor
    fast_grad = grad_embed[1] * embed_factor
    return (proto_grad, slow_grad, fast_grad)


def solution(mesh):
    placed = (P("batch", None), P("batch", None), P("proto", None))
    return jax.shard_map(
        body,
        mesh=mesh,
        in_specs=placed,
        out_specs=(P("proto", None), P("batch", None), P("batch", None)),
        check_vma=False,
    )
```

profile of v0, /device:TPU:1, one launch (start us, length us, event | category | flops | bytes accessed | tf_op | source)
XLA Modules:
  0.0 716.6 jit_solution(129335976540485152)
XLA Ops:
  7.2 0.0 all-reduce.5.cloned.1.call-start
  7.2 1.6 fusion.5
  8.8 1.9 multiply_reduce_fusion.9
  10.7 9.2 %fusion.4 = (f32[2,2048]{1,0:T(2,128)S(1)}, f32[2,1024,2048]{2,1,0:T(8,128)}) fusion(f32[2048,256]{1,0:T(8,128)} %param.5, f32[2048]{0:T(1024)S(1)} %add_sqrt_fusion, f32[2,1024]{1,0:T(2,128)S(1)} %add_sqrt_fusion.1, bf16[1,1024,256]{2,1,0:T(8,128)(2,1)} %bitcast.16, bf16[1,1024,256]{2,1,0:T(8,128)(2,1)} %bitcast.20), kind=kOutput, calls=%fused_computation.15 | convolution fusion | flops 2159013888 | bytes 19955712 | tf_op jit(solution)/shard_map/vbd,kd->vbk/dot_general | solution.py:48
  20.0 48.8 %psum.78 = f32[2,2048]{1,0:T(2,128)S(1)} all-reduce(f32[2,2048]{1,0:T(2,128)S(1)} %get-tuple-element.17), channel_id=1, replica_groups=mesh['batch'=16,'proto'=16] {'batch'}, use_global_device_ids=true, to_apply=%region_5.0 | all-reduce | flops 4096 | bytes 32768 | tf_op jit(solution)/shard_map/psum | solution.py:55
  68.8 9.0 %fusion.3 = (f32[2,1024]{1,0:T(2,128)S(1)}, f32[2,1024]{1,0:T(2,128)S(1)}) fusion(f32[2,1024,2048]{2,1,0:T(8,128)} %get-tuple-element.18, f32[2,2048]{1,0:T(2,128)S(1)} %multiply_divide_fusion.3), kind=kLoop, calls=%fused_computation.12 | loop fusion | flops 20967424 | bytes 16809984 | tf_op jit(solution)/shard_map/reduce_sum | solution.py:51
  77.8 34.0 %psum.79 = f32[2,1024]{1,0:T(2,128)S(1)} all-reduce(f32[2,1024]{1,0:T(2,128)S(1)} %get-tuple-element.4), channel_id=1, replica_groups=mesh['batch'=16,'proto'=16] {'proto'}, use_global_device_ids=true, to_apply=%region_7.0 | all-reduce | flops 2048 | bytes 16384 | tf_op jit(solution)/shard_map/psum | solution.py:23
  111.8 7.4 %multiply_reduce_fusion.2 = f32[2,2048]{1,0:T(2,128)S(1)} fusion(f32[2,1024]{1,0:T(2,128)S(1)} %multiply_divide_fusion.5, f32[2,1024,2048]{2,1,0:T(8,128)} %get-tuple-element.18), kind=kLoop, calls=%fused_computation.5 | loop fusion | flops 12578816 | bytes 16801792 | tf_op jit(solution)/shard_map/reduce_sum | solution.py:55
  119.1 52.9 %psum.80 = f32[2,2048]{1,0:T(2,128)S(1)} all-reduce(f32[2,2048]{1,0:T(2,128)S(1)} %multiply_reduce_fusion.2), channel_id=1, replica_groups=mesh['batch'=16,'proto'=16] {'batch'}, use_global_device_ids=true, to_apply=%region_9.0 | all-reduce | flops 4096 | bytes 32768 | tf_op jit(solution)/shard_map/psum | solution.py:55
  172.0 8.6 %multiply_reduce_fusion.1 = f32[2,1024]{1,0:T(2,128)S(1)} fusion(f32[2,2048]{1,0:T(2,128)S(1)} %multiply_divide_fusion.2, f32[2,1024,2048]{2,1,0:T(8,128)} %get-tuple-element.18), kind=kLoop, calls=%fused_computation.4 | loop fusion | flops 12580864 | bytes 16801792 | tf_op jit(solution)/shard_map/reduce_sum | solution.py:57
  180.6 29.0 %psum.81 = f32[2,1024]{1,0:T(2,128)S(1)} all-reduce(f32[2,1024]{1,0:T(2,128)S(1)} %multiply_reduce_fusion.1), channel_id=1, replica_groups=mesh['batch'=16,'proto'=16] {'proto'}, use_global_device_ids=true, to_apply=%region_11.0 | all-reduce | flops 2048 | bytes 16384 | tf_op jit(solution)/shard_map/psum | solution.py:23
  209.7 7.4 %multiply_reduce_fusion = f32[2,2048]{1,0:T(2,128)S(1)} fusion(f32[2,1024]{1,0:T(2,128)S(1)} %multiply_divide_fusion.4, f32[2,1024,2048]{2,1,0:T(8,128)} %get-tuple-element.18), kind=kLoop, calls=%fused_computation.3 | loop fusion | flops 12578816 | bytes 16801792 | tf_op jit(solution)/shard_map/reduce_sum | solution.py:55
  217.0 52.8 %psum.82 = f32[2,2048]{1,0:T(2,128)S(1)} all-reduce(f32[2,2048]{1,0:T(2,128)S(1)} %multiply_reduce_fusion), channel_id=1, replica_groups=mesh['batch'=16,'proto'=16] {'batch'}, use_global_device_ids=true, to_apply=%region_13.0 | all-reduce | flops 4096 | bytes 32768 | tf_op jit(solution)/shard_map/psum | solution.py:55
  269.9 8.6 %multiply_reduce_fusion.4 = f32[2,1024]{1,0:T(2,128)S(1)} fusion(f32[2,2048]{1,0:T(2,128)S(1)} %multiply_divide_fusion.1, f32[2,1024,2048]{2,1,0:T(8,128)} %get-tuple-element.18), kind=kLoop, calls=%fused_computation.10 | loop fusion | flops 12580864 | bytes 16801792 | tf_op jit(solution)/shard_map/reduce_sum | solution.py:57
  278.5 57.5 %all-reduce.1 = (f32[2,1024]{1,0:T(2,128)S(1)}, f32[2,1024]{1,0:T(2,128)S(1)}) all-reduce(f32[2,1024]{1,0:T(2,128)S(1)} %multiply_reduce_fusion.4, f32[2,1024]{1,0:T(2,128)S(1)} %get-tuple-element.3), channel_id=1, replica_groups=mesh['batch'=16,'proto'=16] {'proto'}, use_global_device_ids=true, to_apply=%region_15.0 | all-reduce | flops 4096 | bytes 32768 | tf_op jit(solution)/shard_map/psum | solution.py:23
  336.0 18.3 %fusion.2 = (f32[2,1024,2048]{2,1,0:T(8,128)}, f32[2,1024,2048]{2,1,0:T(8,128)}) fusion(f32[2,1024,2048]{2,1,0:T(8,128)} %get-tuple-element.18, f32[2,1024]{1,0:T(2,128)S(1)} %get-tuple-element.8, f32[2,1024]{1,0:T(2,128)S(1)} %get-tuple-element.7, f32[2,2048]{1,0:T(2,128)S(1)} %multiply_divide_fusion.1), kind=kLoop, calls=%fused_computation.11 | loop fusion | flops 20971520 | bytes 50364416 | tf_op jit(solution)/shard_map/div | solution.py:64
  354.3 0.0 copy-start.2
  354.3 0.0 copy-start.3
  354.3 19.2 %slice_subtract_fusion.1 = (f32[1,1024,2048]{2,1,0:T(8,128)}, f32[1,1024,2048]{2,1,0:T(8,128)}) fusion(f32[2,1024,2048]{2,1,0:T(8,128)} %get-tuple-element.14, f32[2,1024,2048]{2,1,0:T(8,128)} %get-tuple-element.13), kind=kLoop, calls=%fused_computation.14 | loop fusion | flops 4194304 | bytes 50331648 | tf_op jit(solution)/shard_map/sub | solution.py:65
  373.5 0.0 copy-done.2
  373.5 0.0 copy-done.3
  373.5 0.0 copy-start
  373.5 8.8 %convolution_bitcast_fusion = f32[2048,256]{1,0:T(8,128)} fusion(f32[1,1024,2048]{2,1,0:T(8,128)} %get-tuple-element.12, f32[1,1024,2048]{2,1,0:T(8,128)} %get-tuple-element.11, f32[2,1024]{1,0:T(2,128)S(1)} %add_sqrt_fusion.1, bf16[1,1024,256]{2,1,0:T(8,128)(2,1)S(1)} %bitcast.17, bf16[1,1024,256]{2,1,0:T(8,128)(2,1)S(1)} %bitcast.21), kind=kOutput, calls=%fused_computation.16 | convolution fusion | flops 2162163712 | bytes 19931136 | tf_op jit(solution)/shard_map/vbk,vbd->kd/dot_general | solution.py:68
  382.3 0.0 all-reduce.5.cloned.1.call-update
  382.3 0.3 all-reduce.7.cloned.1.call-start
  382.6 0.0 copy-done
  382.6 8.5 %fusion.11 = f32[2,1024,256]{2,1,0:T(8,128)} fusion(f32[1,1024,2048]{2,1,0:T(8,128)} %get-tuple-element.12, f32[1,1024,2048]{2,1,0:T(8,128)} %get-tuple-element.11, f32[2048,256]{1,0:T(8,128)S(1)} %copy-done, f32[2048]{0:T(1024)S(1)} %add_sqrt_fusion), kind=kOutput, calls=%fused_computation.33 | convolution fusion | flops 2161115136 | bytes 20979712 | tf_op jit(solution)/shard_map/vbk,kd->vbd/dot_general | solution.py:70
  391.1 0.0 all-reduce.7.cloned.1.call-update
  391.2 116.1 %all-reduce.5.cloned.1.call-done = f32[2048,256]{1,0:T(8,128)} async-done(((f32[2048,256]{1,0:T(8,128)}), f32[2048,256]{1,0:T(8,128)}) %all-reduce.5.cloned.1.call-update) | async-done | bytes 2097168 | tf_op jit(solution)/shard_map/psum | solution.py:69
  507.3 2.2 multiply_reduce_fusion.8
  509.5 3.6 multiply_reduce_fusion.7
  513.8 0.0 copy-start.1
  513.8 97.2 %all-reduce.7.cloned.1.call-done = f32[2,1024,256]{2,1,0:T(8,128)} async-done(((f32[2,1024,256]{2,1,0:T(8,128)}), f32[2,1024,256]{2,1,0:T(8,128)}) %all-reduce.7.cloned.1.call-update) | async-done | bytes 2097168 | tf_op jit(solution)/shard_map/psum | solution.py:71
  611.0 15.5 %multiply_reduce_fusion.5 = (f32[]{:T(128)}, f32[2,1024,256]{2,1,0:T(8,128)}) fusion(f32[2,1024,256]{2,1,0:T(8,128)} %all-reduce.7.cloned.1.call-done, f32[2,1024]{1,0:T(2,128)S(1)} %add_sqrt_fusion.1, bf16[1,1024,256]{2,1,0:T(8,128)(2,1)S(1)} %bitcast.18, bf16[1,1024,256]{2,1,0:T(8,128)(2,1)S(1)} %bitcast.22), kind=kOutput, calls=%fused_computation.20 | output fusion | flops 7342334 | bytes 5251076 | tf_op jit(solution)/shard_map/mul | solution.py:19
  627.1 76.8 %all-reduce = (f32[]{:T(128)}, f32[]{:T(128)}) all-reduce(f32[]{:T(128)S(6)} %div.101, f32[]{:T(128)S(6)} %div.104), channel_id=1, replica_groups=mesh['batch'=16,'proto'=16] {'batch','proto'}, use_global_device_ids=true, to_apply=%region_19.0 | all-reduce | flops 2 | bytes 16 | tf_op jit(solution)/shard_map/psum | solution.py:27
  705.3 0.0 copy-done.1
  705.3 1.5 broadcast_multiply_fusion
  706.8 3.0 fusion.9
  (7 shorter events, 0.1 us)
Async XLA Ops:
  7.2 500.1 %all-reduce.5.cloned.1.call-start = ((), (), s32[]{:S(2)}) async-start(), calls=%async_computation | async-start | bytes 4194304 | tf_op jit(solution)/shard_map/psum | solution.py:69
  354.3 19.2 %copy-start.2 = (bf16[1024,256]{1,0:T(8,128)(2,1)S(1)}, bf16[1024,256]{1,0:T(8,128)(2,1)}, u32[]{:S(2)}) copy-start(bf16[1024,256]{1,0:T(8,128)(2,1)} %param.4) | copy-start | bytes 1572868
  354.3 19.2 %copy-start.3 = (bf16[1024,256]{1,0:T(8,128)(2,1)S(1)}, bf16[1024,256]{1,0:T(8,128)(2,1)}, u32[]{:S(2)}) copy-start(bf16[1024,256]{1,0:T(8,128)(2,1)} %param.3) | copy-start | bytes 1572868
  373.5 9.1 %copy-start = (f32[2048,256]{1,0:T(8,128)S(1)}, f32[2048,256]{1,0:T(8,128)}, u32[]{:S(2)}) copy-start(f32[2048,256]{1,0:T(8,128)} %param.5) | copy-start | bytes 6291460
  382.3 228.7 %all-reduce.7.cloned.1.call-start = ((), (), s32[]{:S(2)}) async-start(), calls=%async_computation.1 | async-start | bytes 4194304 | tf_op jit(solution)/shard_map/psum | solution.py:71
  513.8 191.5 %copy-start.1 = (f32[2048,256]{1,0:T(8,128)S(1)}, f32[2048,256]{1,0:T(8,128)}, u32[]{:S(2)}) copy-start(f32[2048,256]{1,0:T(8,128)} %get-tuple-element.10) | copy-start | bytes 6291460
Sparse Core Ops, SparseCore 0:
  382.4 124.8 all-reduce.4
  510.6 100.3 all-reduce.6
where the time goes:
time: 717 us
  blocking collectives  352 us (49%)
  waiting for transfers between devices  213 us (30%)
  other arithmetic  108 us (15%)
  matrix products  26.5 us (4%)
  between operations  16.9 us (2%)
    psum x3, blocking collectives, body(): lax.psum(jnp.sum(code_table * clip_scale[:, :, None], axis=1), 'batch')  155 us
    psum x3, blocking collectives, row_total(): return lax.psum(row_terms, 'proto')  121 us
    psum x1, waiting for transfers between devices, body(): grad_proto_unit = lax.psum(proto_terms, 'batch')  116 us
    psum x1, waiting for transfers between devices, body(): grad_unit = lax.psum(embed_terms, 'proto')  97.2 us
    psum x1, blocking collectives, normalizers(): totals = lax.psum((proto_square, embed_square), ('batch', 'proto'))  76.8 us
    sub x1, other arithmetic, body(): probs[0] - codes[1]  19.2 us
    div x1, other arithmetic, body(): probs = soft_exp / denominator[:, :, None]  18.3 us
    reduce_sum x2, other arithmetic, body(): row_terms = jnp.sum(code_table * proto_scale[:, None, :], axis=2)  17.2 us
  transfers between devices with their start and end apart: 2, of which 2 were waited for; matrix products, arithmetic and copies ran while one was open for 2% of the time, Pallas kernels for 0%

commit v1 on v0

--- a/solution.py
+++ b/solution.py
@@ -7,6 +7,10 @@
 CODE_EPS = 0.05
 TEMPER = 0.1
 NORM_EPS = 1e-06
+
+
+def cards_link(buf, peer_axis, net_axis):
+    return lax.psum(lax.psum(buf, axis_name=peer_axis), axis_name=net_axis)
 
 
 def normalize(raw_rows):
@@ -24,7 +28,7 @@
 
 
 def normalizers(proto_square, embed_square, proto_entries, embed_entries):
-    totals = lax.psum((proto_square, embed_square), ("batch", "proto"))
+    totals = cards_link((proto_square, embed_square), "batch", "proto")
     proto_factor = lax.rsqrt(totals[0] / proto_entries + NORM_EPS)
     embed_factor = lax.rsqrt(totals[1] / embed_entries + NORM_EPS)
     return (proto_factor, embed_factor)

time: 717 us -> 704 us (0.982)
  blocking collectives: 352 us -> 332 us
    psum x1 -> x2, blocking collectives: 76.8 us -> 57.4 us  [cards_link(): return lax.psum(lax.psum(buf, axis_name=peer_axis), axis_name=net_axis)]
where the time goes in v1:
time: 704 us; the launch traced here: 697 us
  blocking collectives  332 us (47%)
  waiting for transfers between devices  213 us (30%)
  other arithmetic  108 us (15%)
  matrix products  26.5 us (4%)
  between operations  16.9 us (2%)
    psum x3, blocking collectives, body(): lax.psum(jnp.sum(code_table * clip_scale[:, :, None], axis=1), 'batch')  155 us
    psum x3, blocking collectives, row_total(): return lax.psum(row_terms, 'proto')  121 us
    psum x1, waiting for transfers between devices, body(): grad_proto_unit = lax.psum(proto_terms, 'batch')  116 us
    psum x1, waiting for transfers between devices, body(): grad_unit = lax.psum(embed_terms, 'proto')  97.2 us
    psum x2, blocking collectives, cards_link(): return lax.psum(lax.psum(buf, axis_name=peer_axis), axis_name=net_axis)  57.4 us
    sub x1, other arithmetic, body(): probs[0] - codes[1]  19.2 us
    div x1, other arithmetic, body(): probs = soft_exp / denominator[:, :, None]  18.3 us
    reduce_sum x2, other arithmetic, body(): row_terms = jnp.sum(code_table * proto_scale[:, None, :], axis=2)  17.2 us
  transfers between devices with their start and end apart: 2, of which 2 were waited for; matrix products, arithmetic and copies ran while one was open for 2% of the time, Pallas kernels for 0%

profile of v1, /device:TPU:1, one launch (start us, length us, event | category | flops | bytes accessed | tf_op | source)
XLA Modules:
  0.0 697.2 jit_solution(8995747704545140042)
XLA Ops:
  7.2 0.0 all-reduce.6.cloned.1.call-start
  7.2 1.6 fusion.5
  8.8 1.9 multiply_reduce_fusion.9
  10.7 9.2 %fusion.4 = (f32[2,2048]{1,0:T(2,128)S(1)}, f32[2,1024,2048]{2,1,0:T(8,128)}) fusion(f32[2048,256]{1,0:T(8,128)} %param.5, f32[2048]{0:T(1024)S(1)} %add_sqrt_fusion, f32[2,1024]{1,0:T(2,128)S(1)} %add_sqrt_fusion.1, bf16[1,1024,256]{2,1,0:T(8,128)(2,1)} %bitcast.16, bf16[1,1024,256]{2,1,0:T(8,128)(2,1)} %bitcast.20), kind=kOutput, calls=%fused_computation.15 | convolution fusion | flops 2159013888 | bytes 19955712 | tf_op jit(solution)/shard_map/vbd,kd->vbk/dot_general | solution.py:52
  20.0 48.8 %psum.92 = f32[2,2048]{1,0:T(2,128)S(1)} all-reduce(f32[2,2048]{1,0:T(2,128)S(1)} %get-tuple-element.19), channel_id=1, replica_groups=mesh['batch'=16,'proto'=16] {'batch'}, use_global_device_ids=true, to_apply=%region_5.0 | all-reduce | flops 4096 | bytes 32768 | tf_op jit(solution)/shard_map/psum | solution.py:59
  68.8 9.0 %fusion.3 = (f32[2,1024]{1,0:T(2,128)S(1)}, f32[2,1024]{1,0:T(2,128)S(1)}) fusion(f32[2,1024,2048]{2,1,0:T(8,128)} %get-tuple-element.20, f32[2,2048]{1,0:T(2,128)S(1)} %multiply_divide_fusion.3), kind=kLoop, calls=%fused_computation.12 | loop fusion | flops 20967424 | bytes 16809984 | tf_op jit(solution)/shard_map/reduce_sum | solution.py:55
  77.8 34.0 %psum.93 = f32[2,1024]{1,0:T(2,128)S(1)} all-reduce(f32[2,1024]{1,0:T(2,128)S(1)} %get-tuple-element.4), channel_id=1, replica_groups=mesh['batch'=16,'proto'=16] {'proto'}, use_global_device_ids=true, to_apply=%region_7.0 | all-reduce | flops 2048 | bytes 16384 | tf_op jit(solution)/shard_map/psum | solution.py:27
  111.8 7.4 %multiply_reduce_fusion.2 = f32[2,2048]{1,0:T(2,128)S(1)} fusion(f32[2,1024]{1,0:T(2,128)S(1)} %multiply_divide_fusion.5, f32[2,1024,2048]{2,1,0:T(8,128)} %get-tuple-element.20), kind=kLoop, calls=%fused_computation.5 | loop fusion | flops 12578816 | bytes 16801792 | tf_op jit(solution)/shard_map/reduce_sum | solution.py:59
  119.1 52.9 %psum.94 = f32[2,2048]{1,0:T(2,128)S(1)} all-reduce(f32[2,2048]{1,0:T(2,128)S(1)} %multiply_reduce_fusion.2), channel_id=1, replica_groups=mesh['batch'=16,'proto'=16] {'batch'}, use_global_device_ids=true, to_apply=%region_9.0 | all-reduce | flops 4096 | bytes 32768 | tf_op jit(solution)/shard_map/psum | solution.py:59
  172.0 8.6 %multiply_reduce_fusion.1 = f32[2,1024]{1,0:T(2,128)S(1)} fusion(f32[2,2048]{1,0:T(2,128)S(1)} %multiply_divide_fusion.2, f32[2,1024,2048]{2,1,0:T(8,128)} %get-tuple-element.20), kind=kLoop, calls=%fused_computation.4 | loop fusion | flops 12580864 | bytes 16801792 | tf_op jit(solution)/shard_map/reduce_sum | solution.py:61
  180.6 29.0 %psum.95 = f32[2,1024]{1,0:T(2,128)S(1)} all-reduce(f32[2,1024]{1,0:T(2,128)S(1)} %multiply_reduce_fusion.1), channel_id=1, replica_groups=mesh['batch'=16,'proto'=16] {'proto'}, use_global_device_ids=true, to_apply=%region_11.0 | all-reduce | flops 2048 | bytes 16384 | tf_op jit(solution)/shard_map/psum | solution.py:27
  209.7 7.4 %multiply_reduce_fusion = f32[2,2048]{1,0:T(2,128)S(1)} fusion(f32[2,1024]{1,0:T(2,128)S(1)} %multiply_divide_fusion.4, f32[2,1024,2048]{2,1,0:T(8,128)} %get-tuple-element.20), kind=kLoop, calls=%fused_computation.3 | loop fusion | flops 12578816 | bytes 16801792 | tf_op jit(solution)/shard_map/reduce_sum | solution.py:59
  217.0 52.8 %psum.96 = f32[2,2048]{1,0:T(2,128)S(1)} all-reduce(f32[2,2048]{1,0:T(2,128)S(1)} %multiply_reduce_fusion), channel_id=1, replica_groups=mesh['batch'=16,'proto'=16] {'batch'}, use_global_device_ids=true, to_apply=%region_13.0 | all-reduce | flops 4096 | bytes 32768 | tf_op jit(solution)/shard_map/psum | solution.py:59
  269.9 8.6 %multiply_reduce_fusion.4 = f32[2,1024]{1,0:T(2,128)S(1)} fusion(f32[2,2048]{1,0:T(2,128)S(1)} %multiply_divide_fusion.1, f32[2,1024,2048]{2,1,0:T(8,128)} %get-tuple-element.20), kind=kLoop, calls=%fused_computation.10 | loop fusion | flops 12580864 | bytes 16801792 | tf_op jit(solution)/shard_map/reduce_sum | solution.py:61
  278.5 57.5 %all-reduce.1 = (f32[2,1024]{1,0:T(2,128)S(1)}, f32[2,1024]{1,0:T(2,128)S(1)}) all-reduce(f32[2,1024]{1,0:T(2,128)S(1)} %multiply_reduce_fusion.4, f32[2,1024]{1,0:T(2,128)S(1)} %get-tuple-element.3), channel_id=1, replica_groups=mesh['batch'=16,'proto'=16] {'proto'}, use_global_device_ids=true, to_apply=%region_15.0 | all-reduce | flops 4096 | bytes 32768 | tf_op jit(solution)/shard_map/psum | solution.py:27
  336.0 18.3 %fusion.2 = (f32[2,1024,2048]{2,1,0:T(8,128)}, f32[2,1024,2048]{2,1,0:T(8,128)}) fusion(f32[2,1024,2048]{2,1,0:T(8,128)} %get-tuple-element.20, f32[2,1024]{1,0:T(2,128)S(1)} %get-tuple-element.8, f32[2,1024]{1,0:T(2,128)S(1)} %get-tuple-element.7, f32[2,2048]{1,0:T(2,128)S(1)} %multiply_divide_fusion.1), kind=kLoop, calls=%fused_computation.11 | loop fusion | flops 20971520 | bytes 50364416 | tf_op jit(solution)/shard_map/div | solution.py:68
  354.3 0.0 copy-start.2
  354.3 0.0 copy-start.3
  354.3 19.2 %slice_subtract_fusion.1 = (f32[1,1024,2048]{2,1,0:T(8,128)}, f32[1,1024,2048]{2,1,0:T(8,128)}) fusion(f32[2,1024,2048]{2,1,0:T(8,128)} %get-tuple-element.16, f32[2,1024,2048]{2,1,0:T(8,128)} %get-tuple-element.15), kind=kLoop, calls=%fused_computation.14 | loop fusion | flops 4194304 | bytes 50331648 | tf_op jit(solution)/shard_map/sub | solution.py:69
  373.5 0.0 copy-done.2
  373.5 0.0 copy-done.3
  373.5 0.0 copy-start
  373.5 8.8 %convolution_bitcast_fusion = f32[2048,256]{1,0:T(8,128)} fusion(f32[1,1024,2048]{2,1,0:T(8,128)} %get-tuple-element.14, f32[1,1024,2048]{2,1,0:T(8,128)} %get-tuple-element.13, f32[2,1024]{1,0:T(2,128)S(1)} %add_sqrt_fusion.1, bf16[1,1024,256]{2,1,0:T(8,128)(2,1)S(1)} %bitcast.17, bf16[1,1024,256]{2,1,0:T(8,128)(2,1)S(1)} %bitcast.21), kind=kOutput, calls=%fused_computation.16 | convolution fusion | flops 2162163712 | bytes 19931136 | tf_op jit(solution)/shard_map/vbk,vbd->kd/dot_general | solution.py:72
  382.3 0.0 all-reduce.6.cloned.1.call-update
  382.3 0.3 all-reduce.8.cloned.1.call-start
  382.6 0.0 copy-done
  382.6 8.5 %fusion.11 = f32[2,1024,256]{2,1,0:T(8,128)} fusion(f32[1,1024,2048]{2,1,0:T(8,128)} %get-tuple-element.14, f32[1,1024,2048]{2,1,0:T(8,128)} %get-tuple-element.13, f32[2048,256]{1,0:T(8,128)S(1)} %copy-done, f32[2048]{0:T(1024)S(1)} %add_sqrt_fusion), kind=kOutput, calls=%fused_computation.33 | convolution fusion | flops 2161115136 | bytes 20979712 | tf_op jit(solution)/shard_map/vbk,kd->vbd/dot_general | solution.py:74
  391.1 0.0 all-reduce.8.cloned.1.call-update
  391.2 116.1 %all-reduce.6.cloned.1.call-done = f32[2048,256]{1,0:T(8,128)} async-done(((f32[2048,256]{1,0:T(8,128)}), f32[2048,256]{1,0:T(8,128)}) %all-reduce.6.cloned.1.call-update) | async-done | bytes 2097168 | tf_op jit(solution)/shard_map/psum | solution.py:73
  507.3 2.2 multiply_reduce_fusion.8
  509.5 3.6 multiply_reduce_fusion.7
  513.8 0.0 copy-start.1
  513.8 97.2 %all-reduce.8.cloned.1.call-done = f32[2,1024,256]{2,1,0:T(8,128)} async-done(((f32[2,1024,256]{2,1,0:T(8,128)}), f32[2,1024,256]{2,1,0:T(8,128)}) %all-reduce.8.cloned.1.call-update) | async-done | bytes 2097168 | tf_op jit(solution)/shard_map/psum | solution.py:75
  611.0 15.5 %multiply_reduce_fusion.5 = (f32[]{:T(128)}, f32[2,1024,256]{2,1,0:T(8,128)}) fusion(f32[2,1024,256]{2,1,0:T(8,128)} %all-reduce.8.cloned.1.call-done, f32[2,1024]{1,0:T(2,128)S(1)} %add_sqrt_fusion.1, bf16[1,1024,256]{2,1,0:T(8,128)(2,1)S(1)} %bitcast.18, bf16[1,1024,256]{2,1,0:T(8,128)(2,1)S(1)} %bitcast.22), kind=kOutput, calls=%fused_computation.20 | output fusion | flops 7342334 | bytes 5251076 | tf_op jit(solution)/shard_map/mul | solution.py:23
  627.1 25.9 %all-reduce.2 = (f32[]{:T(128)}, f32[]{:T(128)}) all-reduce(f32[]{:T(128)S(6)} %div.101, f32[]{:T(128)S(6)} %div.104), channel_id=1, replica_groups=mesh['batch'=16,'proto'=16] {'batch'}, use_global_device_ids=true, to_apply=%region_19.0 | all-reduce | flops 2 | bytes 16 | tf_op jit(solution)/shard_map/psum | solution.py:13
  653.0 31.5 %all-reduce = (f32[]{:T(128)}, f32[]{:T(128)}) all-reduce(f32[]{:T(128)} %get-tuple-element.9, f32[]{:T(128)} %get-tuple-element.10), channel_id=1, replica_groups=mesh['batch'=16,'proto'=16] {'proto'}, use_global_device_ids=true, to_apply=%region_20.0 | all-reduce | flops 2 | bytes 16 | tf_op jit(solution)/shard_map/psum | solution.py:13
  685.9 0.0 copy-done.1
  685.9 1.5 broadcast_multiply_fusion
  687.4 3.0 fusion.9
  (7 shorter events, 0.1 us)
Async XLA Ops:
  7.2 500.1 %all-reduce.6.cloned.1.call-start = ((), (), s32[]{:S(2)}) async-start(), calls=%async_computation | async-start | bytes 4194304 | tf_op jit(solution)/shard_map/psum | solution.py:73
  354.3 19.2 %copy-start.2 = (bf16[1024,256]{1,0:T(8,128)(2,1)S(1)}, bf16[1024,256]{1,0:T(8,128)(2,1)}, u32[]{:S(2)}) copy-start(bf16[1024,256]{1,0:T(8,128)(2,1)} %param.4) | copy-start | bytes 1572868
  354.3 19.2 %copy-start.3 = (bf16[1024,256]{1,0:T(8,128)(2,1)S(1)}, bf16[1024,256]{1,0:T(8,128)(2,1)}, u32[]{:S(2)}) copy-start(bf16[1024,256]{1,0:T(8,128)(2,1)} %param.3) | copy-start | bytes 1572868
  373.5 9.1 %copy-start = (f32[2048,256]{1,0:T(8,128)S(1)}, f32[2048,256]{1,0:T(8,128)}, u32[]{:S(2)}) copy-start(f32[2048,256]{1,0:T(8,128)} %param.5) | copy-start | bytes 6291460
  382.3 228.7 %all-reduce.8.cloned.1.call-start = ((), (), s32[]{:S(2)}) async-start(), calls=%async_computation.1 | async-start | bytes 4194304 | tf_op jit(solution)/shard_map/psum | solution.py:75
  513.8 172.1 %copy-start.1 = (f32[2048,256]{1,0:T(8,128)S(1)}, f32[2048,256]{1,0:T(8,128)}, u32[]{:S(2)}) copy-start(f32[2048,256]{1,0:T(8,128)} %get-tuple-element.12) | copy-start | bytes 6291460
Sparse Core Ops, SparseCore 0:
  382.4 124.8 all-reduce.5
  510.6 100.3 all-reduce.7
